TPU v7x, 32 devices: a whole 2x2x4 slice. The times are simulated.
32 devices in a mesh: island: 4 (over y, core), inner: 8 (over z, x).
Axes of the slice: x: 2, y: 2, z: 4, core: 2. Of those that a mesh axis runs over, the one named last changes fastest.
Arguments:
- particles: float32 [384, 128, 128], P(('island', 'inner')), may hold values from -6 to 6
- velocity_x: float32 [128, 128], replicated, may hold values from -1 to 1
- velocity_y: float32 [128, 128], replicated, may hold values from -1 to 1
- copy_lists: int32 [1, 1, 384], P(None, None, ('island', 'inner')), may hold values from 0 to 95, as said below
- migrants: int32 [1, 384], P(None, ('island', 'inner')), may hold values from 0 to 3
- noise: float32 [1, 1, 384, 4096], P(None, None, ('island', 'inner')), may hold values from -6 to 6
Outputs:
- final_states: float32 [384, 128, 128], P(('island', 'inner'))
Inputs may be any that keep to these rules, and one draw needn't show every extreme that they name: copy_lists[c, r, k] counts particles within the slot's island. Group each island's particles into blocks of 12 in order (block j holds positions j * 12 to (j + 1) * 12 - 1); the 12 slots of one such block copy at most 2 distinct particles of any one block, and in every round some block of slots copies exactly 2 distinct particles of one block.
All inputs are finite; a program needn't handle non-finite values.
Results may differ from a plain program's by a relative error of at most 0.00002.
Values sent between devices are 32-bit elements; how exact they have to be, the bound alone decides.
A program may use at most 128 MiB of HBM per device.

v0:
```python
import jax
import jax.numpy as jnp
from jax import lax
from jax.sharding import PartitionSpec as P

G = 128
CAP = 2
STEPS = 6


diffusion = 0.2
advection = 0.1
noise_gain = 0.3


def stencil(field, velocity_x, velocity_y):
    east = jnp.roll(field, -1, 1)
    west = jnp.roll(field, 1, 1)
    north = jnp.roll(field, -1, 2)
    south = jnp.roll(field, 1, 2)
    laplace = east + west + north + south - 4.0 * field
    transport = (velocity_x + field) * (east - west) + (velocity_y + field) * (north - south)
    return field + diffusion * laplace - advection * transport


def upsample(coarse):
    count = coarse.shape[0]
    half = G // 2
    shaped = coarse.reshape(count, half, 1, half, 1)
    return jnp.broadcast_to(shaped, (count, half, 2, half, 2)).reshape(count, G, G)


def select_rows(carry, piece, wanted):
    rows = piece.shape[0]
    inside = (wanted >= 0) & (wanted < rows)
    taken = jnp.take(piece, jnp.clip(wanted, 0, rows - 1), axis=0)
    return jnp.where(inside[:, None, None], taken, carry)


def copy_direct(states, wanted, requests):
    inner_count = lax.axis_size("inner")
    myself = lax.axis_index("inner")
    local_count = states.shape[0]
    asked = requests.reshape(inner_count, local_count)
    own_ids = myself * local_count + jnp.arange(local_count, dtype=jnp.int32)
    needed = jnp.any(asked[:, :, None] == own_ids[None, None, :], axis=1)
    order = jnp.cumsum(needed.astype(jnp.int32), axis=1) - 1
    places = jnp.arange(CAP, dtype=jnp.int32)
    marked = (order[:, None, :] == places[None, :, None]) & needed[:, None, :]
    send_index = jnp.sum(
        marked.astype(jnp.int32) * jnp.arange(local_count, dtype=jnp.int32)[None, None, :], axis=2
    )
    outgoing = jnp.take(states, send_index, axis=0)
    incoming = lax.all_to_all(outgoing, "inner", split_axis=0, concat_axis=0, tiled=True)
    every_id = jnp.arange(inner_count * local_count, dtype=jnp.int32).reshape(
        inner_count, local_count
    )
    mine_needed = jnp.any(wanted[:, None, None] == every_id[None, :, :], axis=0)
    mine_order = jnp.cumsum(mine_needed.astype(jnp.int32), axis=1) - 1
    source_dev = wanted // local_count
    source_local = wanted % local_count
    position = source_dev * CAP + mine_order[source_dev, source_local]
    flat = incoming.reshape(inner_count * CAP, states.shape[1], states.shape[2])
    return jnp.take(flat, position, axis=0)


def body(particles, velocity_x, velocity_y, copy_lists, migrants, noise):
    states = particles
    local_count = states.shape[0]
    all_requests = lax.all_gather(copy_lists, "inner", axis=2, tiled=True)
    wanted = copy_lists[0, 0]
    states = copy_direct(states, wanted, all_requests[0, 0])
    states = states + noise_gain * upsample(noise[0, 0])
    for step in range(STEPS):
        states = stencil(states, velocity_x, velocity_y)
    target = migrants[0] * local_count + jnp.arange(local_count, dtype=jnp.int32)
    return select_rows(
        jnp.zeros_like(states), lax.all_gather(states, "island", axis=0, tiled=True), target
    )


def solution(mesh):
    placed = (
        P(("island", "inner"), None, None),
        P(),
        P(),
        P(None, None, ("island", "inner")),
        P(None, ("island", "inner")),
        P(None, None, ("island", "inner"), None),
    )
    return jax.shard_map(
        body,
        mesh=mesh,
        in_specs=placed,
        out_specs=P(("island", "inner"), None, None),
        check_vma=False,
    )
```

profile of v0, /device:TPU:11, one launch (start us, length us, event | category | flops | bytes accessed | tf_op | source)
XLA Modules:
  0.0 101.6 jit_solution(9488620322474526173)
XLA Ops:
  6.5 0.0 copy-start
  6.5 1.3 %dynamic-slice = u32[1]{0:T(128)} dynamic-slice(u32[32]{0:T(128)} %constant.115, u32[]{:T(128)S(6)} %add.375), dynamic_slice_sizes={1} | dynamic-slice | bytes 12
  8.5 0.8 bitcast_dynamic-update-slice_fusion
  9.3 7.9 %all-reduce = s32[96]{0:T(128)S(1)} all-reduce(s32[96]{0:T(128)S(1)} %bitcast_dynamic-update-slice_fusion), channel_id=1, replica_groups=mesh['island'=4,'inner'=8] {'inner'}, use_global_device_ids=true, to_apply=%add | all-reduce | flops 96 | bytes 768
  17.1 0.1 eq.46
  17.2 0.1 copy.17
  17.3 0.1 compare_reduce_fusion
  17.4 0.2 reduce_window_sum.18
  17.6 0.1 select_reduce_fusion
  17.7 0.1 copy.19
  17.8 0.1 reshape.236
  17.9 0.1 copy.18
  18.0 0.0 copy-done
  18.0 0.0 copy-start.3
  18.0 0.6 gather_fusion.1
  18.6 1.1 %broadcast_select_fusion = f32[8,2,128,128]{3,2,1,0:T(8,128)} fusion(f32[8,2,128,128]{3,2,1,0:T(8,128)S(1)} %bitcast.50, pred[8,2]{1,0:T(8,128)(4,1)S(1)} %copy.18), kind=kLoop, calls=%fused_computation.36 | loop fusion | flops 262144 | bytes 2097168 | tf_op jit(solution)/shard_map/jit(_take)/select_n | solution.py:53
  19.8 5.1 %all-to-all-start = ((f32[8,2,128,128]{3,2,1,0:T(8,128)}), f32[8,2,128,128]{3,2,1,0:T(8,128)}, u32[]{:S(2)}, u32[]{:S(2)}) async-start(f32[8,2,128,128]{3,2,1,0:T(8,128)} %broadcast_select_fusion), calls=%async_computation | async-start | bytes 2097152 | tf_op jit(solution)/shard_map/all_to_all | solution.py:54
  24.9 0.0 all-gather.2.cloned.1.call-start
  24.9 0.0 copy-done.3
  24.9 0.2 broadcast_multiply_fusion
  25.1 0.8 copy.22
  25.9 4.7 %broadcast_in_dim.43 = f32[12,64,2,64,2]{0,4,3,2,1:T(2,128)} broadcast(f32[12,64,64]{0,2,1:T(8,128)S(1)} %bitcast.49), dimensions={0,1,3} | broadcast | bytes 983040 | tf_op jit(solution)/shard_map/broadcast_in_dim | solution.py:30
  30.6 5.3 %copy.21 = f32[12,128,128]{2,1,0:T(8,128)S(1)} copy(f32[12,128,128]{0,2,1:T(8,128)} %bitcast.48) | data formatting | bytes 1572864 | tf_op jit(solution)/shard_map/mul | solution.py:73
  36.0 0.0 copy-done.4
  36.0 0.1 compare_reduce_fusion.1
  36.1 0.2 reduce_window_sum.17
  36.3 0.7 gather_fusion
  37.0 10.1 %all-to-all-done = f32[8,2,128,128]{3,2,1,0:T(8,128)} async-done(((f32[8,2,128,128]{3,2,1,0:T(8,128)}), f32[8,2,128,128]{3,2,1,0:T(8,128)}, u32[]{:S(2)}, u32[]{:S(2)}) %all-to-all-start) | async-done | bytes 1048608 | tf_op jit(solution)/shard_map/all_to_all | solution.py:54
  47.0 1.8 %gather_fusion.2 = f32[12,128,128]{2,1,0:T(8,128)S(1)} fusion(f32[16,128,128]{2,1,0:T(8,128)} %bitcast.9, s32[1024]{0:T(1024)S(1)} %pad_clamp_fusion.1), kind=kCustom, calls=%fused_computation.2 | custom fusion | bytes 1572912 | tf_op jit(solution)/shard_map/jit(_take)/gather | solution.py:64
  48.9 0.1 select_add_fusion
  49.0 0.3 fusion.34
  49.3 0.0 copy-start.1
  49.3 0.0 copy-start.2
  49.3 0.3 fusion.35
  49.6 0.1 fusion.32
  49.8 0.4 copy-done.1
  50.1 0.0 copy-done.2
  50.2 0.8 multiply_subtract_fusion.5
  50.9 0.3 fusion.30
  51.2 0.3 fusion.31
  51.5 0.1 fusion.28
  51.7 0.8 multiply_subtract_fusion.4
  52.4 0.3 fusion.26
  52.7 0.3 fusion.27
  53.0 0.1 fusion.24
  53.2 0.8 multiply_subtract_fusion.3
  53.9 0.3 fusion.22
  54.2 0.3 fusion.23
  54.5 0.1 fusion.20
  54.7 0.8 multiply_subtract_fusion.2
  55.4 0.3 fusion.18
  55.7 0.3 fusion.19
  56.0 0.1 fusion.16
  56.2 0.8 multiply_subtract_fusion.1
  57.0 0.3 fusion.14
  57.2 0.3 fusion.15
  57.5 0.1 fusion.12
  57.7 0.0 copy-start.5
  57.7 1.6 %multiply_subtract_fusion = f32[12,128,128]{2,1,0:T(8,128)} fusion(f32[12,128,128]{2,1,0:T(8,128)S(1)} %multiply_subtract_fusion.1, f32[12,128,127]{2,1,0:T(8,128)S(1)} %get-tuple-element.12, f32[12,128,1]{2,1,0:T(8,128)S(1)} %get-tuple-element.14, f32[12,128,1]{2,1,0:T(8,128)S(1)} %get-tuple-element.13, f32[12,128,127]{2,1,0:T(8,128)S(1)} %get-tuple-element.11, ...), kind=kLoop, calls=%fused_computation.29 | loop fusion | flops 3932160 | bytes 4849664 | tf_op jit(solution)/shard_map/sub | solution.py:23
  59.3 0.0 all-gather.2.cloned.1.call-update
  59.4 0.0 copy-done.5
  59.4 31.8 %all-gather.2.cloned.1.call-done = f32[48,128,128]{2,1,0:T(8,128)} async-done(((f32[12,128,128]{2,1,0:T(8,128)}), f32[48,128,128]{2,1,0:T(8,128)}) %all-gather.2.cloned.1.call-update) | async-done | bytes 3145744 | tf_op jit(solution)/shard_map/all_gather | solution.py:78
  91.3 2.5 %gather_fusion.3 = f32[12,128,128]{2,1,0:T(8,128)S(1)} fusion(f32[48,128,128]{2,1,0:T(8,128)} %all-gather.2.cloned.1.call-done, s32[1024]{0:T(1024)S(1)} %pad_clamp_fusion), kind=kCustom, calls=%fused_computation.3 | custom fusion | bytes 1572912 | tf_op jit(solution)/shard_map/jit(_take)/gather | solution.py:36
  93.8 1.0 %select_select_fusion = f32[12,128,128]{2,1,0:T(8,128)} fusion(f32[12,128,128]{2,1,0:T(8,128)S(1)} %gather_fusion.3, pred[12]{0:T(512)(128)(4,1)S(1)} %get-tuple-element.56, pred[12]{0:T(512)(128)(4,1)S(1)} %get-tuple-element.55), kind=kLoop, calls=%fused_computation.28 | loop fusion | flops 393216 | bytes 1572888 | tf_op jit(solution)/shard_map/jit(_where)/select_n | solution.py:37
  (24 shorter events, 0.2 us)
Async XLA Ops:
  6.5 11.5 %copy-start = (f32[12,128,128]{2,1,0:T(8,128)S(1)}, f32[12,128,128]{2,1,0:T(8,128)}, u32[]{:S(2)}) copy-start(f32[12,128,128]{2,1,0:T(8,128)} %param.6) | copy-start | bytes 2359300
  18.0 6.9 %copy-start.3 = (f32[1,1,12,4096]{3,1,2,0:T(1,128)S(1)}, f32[1,1,12,4096]{3,1,2,0:T(1,128)}, u32[]{:S(2)}) copy-start(f32[1,1,12,4096]{3,1,2,0:T(1,128)} %param.11) | copy-start | bytes 589828
  19.8 27.3 %all-to-all-start = ((f32[8,2,128,128]{3,2,1,0:T(8,128)}), f32[8,2,128,128]{3,2,1,0:T(8,128)}, u32[]{:S(2)}, u32[]{:S(2)}) async-start(f32[8,2,128,128]{3,2,1,0:T(8,128)} %broadcast_select_fusion), calls=%async_computation | async-start | bytes 2097152 | tf_op jit(solution)/shard_map/all_to_all | solution.py:54
  24.9 66.4 %all-gather.2.cloned.1.call-start = ((), (), s32[]{:S(2)}) async-start(), calls=%async_computation.1 | async-start | bytes 3932160 | tf_op jit(solution)/shard_map/all_gather | solution.py:78
  30.6 5.3 %copy-start.4 = (s32[1,1,12]{2,1,0:T(1,128)S(1)}, s32[1,1,12]{2,1,0:T(1,128)}, u32[]{:S(2)}) copy-start(s32[1,1,12]{2,1,0:T(1,128)} %param.9) | copy-start | bytes 148
  49.3 0.8 copy-start.1
  49.3 0.9 copy-start.2
  57.7 1.7 %copy-start.5 = (s32[1,12]{1,0:T(1,128)S(1)}, s32[1,12]{1,0:T(1,128)}, u32[]{:S(2)}) copy-start(s32[1,12]{1,0:T(1,128)} %param.10) | copy-start | bytes 148
Sparse Core Ops, SparseCore 0:
  59.5 31.7 all-gather.1
where the time goes:
time: 103 us; the launch traced here: 102 us
  waiting for transfers between devices  41.9 us (41%)
  local copies, waits for them, and re-layouts  23.6 us (23%)
  between operations  14.4 us (14%)
  other arithmetic  8.73 us (8%)
  blocking collectives  7.86 us (8%)
  starting transfers between devices  5.13 us (5%)
    all_gather x1, waiting for transfers between devices, body(): lax.all_gather(states, 'island', axis=0, tiled=True)  31.8 us
    all_to_all x1, waiting for transfers between devices, copy_direct(): lax.all_to_all(outgoing, 'inner', split_axis=0, concat_axis=0, tiled=True)  10.1 us
    unnamed x1, blocking collectives  7.86 us
    mul x2, local copies, waits for them, and re-layouts, body(): states = states + noise_gain * upsample(noise[0, 0])  6.07 us
    sub x6, other arithmetic, stencil(): return field + diffusion * laplace - advection * transport  5.43 us
    all_to_all x1, starting transfers between devices, copy_direct(): lax.all_to_all(outgoing, 'inner', split_axis=0, concat_axis=0, tiled=True)  5.13 us
    broadcast_in_dim x1, local copies, waits for them, and re-layouts, upsample(): jnp.broadcast_to(shaped, (count, half, 2, half, 2)).reshape(count, G, G)  4.73 us
    slice x12, local copies, waits for them, and re-layouts, stencil(): north = jnp.roll(field, -1, 2)  3.43 us
  transfers between devices with their start and end apart: 2, of which 2 were waited for; matrix products, arithmetic and copies ran while one was open for 12% of the time, Pallas kernels for 0%

commit v1 on v0

v1 whole, which is shorter than its diff:
```python
import functools

import jax
import jax.numpy as jnp
from jax import lax
from jax.experimental import pallas as pl
from jax.experimental.pallas import tpu as pltpu
from jax.sharding import PartitionSpec as P

CAP = 2
STEPS = 6
HALO = 8
CHUNKS = 4
GROUPS = 3
CORES = 2

diffusion = 0.2
advection = 0.1
noise_gain = 0.3

MESH = pl.DeviceIdType.MESH


def windows_of(grid):
    rows = grid // CHUNKS
    wins = [(HALO, 2 * rows - HALO, 1)]
    for c in range(2, CHUNKS):
        wins.append((wins[-1][1], (c + 1) * rows - HALO, c))
    wins[-1] = (wins[-1][0], grid + HALO, CHUNKS - 1)
    return wins


def pieces(first, last, size, grid):
    found = []
    row = first
    while row < last:
        wrapped = row % grid
        stop = min(last, row + size - wrapped % size)
        found.append((wrapped, wrapped + stop - row))
        row = stop
    return found


def join(parts):
    return parts[0] if len(parts) == 1 else jnp.concatenate(parts, axis=0)


def kernel(n_in, n_is, count, grid, *refs):
    lists, migr, part_hbm, vx_ref, vy_ref, noise_hbm, out_hbm = refs[:7]
    part, nz, up, req, send, vel, outv, pos = refs[7:15]
    rest = list(refs[15:])
    recv = rest[:CHUNKS]
    rest = rest[CHUNKS:]
    wins = windows_of(grid)
    n_win = len(wins)
    gath = [rest[w * GROUPS:(w + 1) * GROUPS] for w in range(n_win)]
    rest = rest[n_win * GROUPS:]
    (load_sem, req_send, req_recv, p_send, p_recv, y_send, y_recv,
     c_send, c_recv, f_send, f_recv, out_sem) = rest
    per = count // GROUPS
    rows = grid // CHUNKS
    n_y = n_is // CORES

    me = lax.axis_index("inner")
    isl = lax.axis_index("island")
    my_y = isl // CORES
    core = isl % CORES
    mate = my_y * CORES + (1 - core)

    def inner_of(o):
        return lax.rem(me + o, n_in)

    def y_of(o):
        return lax.rem(my_y + o, n_y) * CORES + core

    barrier = pltpu.get_barrier_semaphore()
    for o in range(1, n_in):
        pl.semaphore_signal(barrier, inc=1, device_id={"inner": inner_of(o)}, device_id_type=MESH)
    for o in range(1, n_y):
        pl.semaphore_signal(barrier, inc=1, device_id={"island": y_of(o)}, device_id_type=MESH)
    pl.semaphore_signal(barrier, inc=1, device_id={"island": mate}, device_id_type=MESH)

    load_part = pltpu.make_async_copy(part_hbm, part, load_sem.at[0])
    load_nz = pltpu.make_async_copy(noise_hbm, nz, load_sem.at[1])
    load_part.start()
    load_nz.start()

    lane = lax.broadcasted_iota(jnp.int32, (1, 128), 1)
    ids = [lists[0, q] for q in range(count)]
    row = jnp.full((1, 128), -1, jnp.int32)
    for q in range(count):
        row = jnp.where(lane == q, ids[q], row)
    req[me] = row

    pl.semaphore_wait(barrier, n_in - 1 + n_y - 1 + 1)

    def req_copy(o):
        return pltpu.make_async_remote_copy(
            src_ref=req.at[me], dst_ref=req.at[me],
            send_sem=req_send.at[o], recv_sem=req_recv.at[o],
            device_id={"inner": inner_of(o)}, device_id_type=MESH)

    def part_copy(c, o):
        return pltpu.make_async_remote_copy(
            src_ref=send.at[o - 1, :, pl.ds(c * rows, rows)],
            dst_ref=recv[c].at[pl.ds(CAP * me, CAP)],
            send_sem=p_send.at[c, o], recv_sem=p_recv.at[c, o],
            device_id={"inner": inner_of(o)}, device_id_type=MESH)

    for o in range(1, n_in):
        req_copy(o).start()

    def wanted(device):
        local = req[device] - me * count
        inside = (local >= 0) & (local < count)
        low = jnp.min(jnp.where(inside, local, count))
        high = jnp.max(jnp.where(inside, local, 0))
        return jnp.minimum(low, high), high

    for q in range(count):
        block = ids[q] // count
        later = jnp.int32(0)
        for other in range(count):
            if other != q:
                hit = (ids[other] >= block * count) & (ids[other] < ids[q])
                later = jnp.maximum(later, hit.astype(jnp.int32))
        pos[q] = block * CAP + later

    load_part.wait()
    low, high = wanted(me)
    for k, which in enumerate((low, high)):
        for c in range(CHUNKS):
            recv[c][CAP * me + k] = part[which, c * rows:(c + 1) * rows, :]

    for o in range(1, n_in):
        req_copy(n_in - o).wait_recv()
        low, high = wanted(inner_of(o))
        send[o - 1, 0] = part[low]
        send[o - 1, 1] = part[high]
        part_copy(0, o).start()
    for c in range(1, CHUNKS):
        for o in range(1, n_in):
            part_copy(c, o).start()

    vel[0] = advection * vx_ref[...]
    vel[1] = advection * vy_ref[...]
    load_nz.wait()
    from_lane = lax.broadcasted_iota(jnp.int32, (128, 128), 0)
    to_lane = lax.broadcasted_iota(jnp.int32, (128, 128), 1)
    spread = [(from_lane == half * 64 + to_lane // 2).astype(jnp.float32) for half in (0, 1)]
    packed = nz.shape[1]

    def upsample(q, carry):
        for half in (0, 1):
            wide = noise_gain * jnp.dot(
                nz[q], spread[half], precision=lax.Precision.HIGHEST,
                preferred_element_type=jnp.float32)
            for k in (0, 1):
                up[q, pl.ds(2 * half + k, packed, stride=4), :] = wide
        return carry

    lax.fori_loop(0, count, upsample, 0)

    def y_copy(w, g, o):
        mine = gath[w][g].at[pl.ds(isl * per, per)]
        return pltpu.make_async_remote_copy(
            src_ref=mine, dst_ref=mine,
            send_sem=y_send.at[w, g, o], recv_sem=y_recv.at[w, g, o],
            device_id={"island": y_of(o)}, device_id_type=MESH)

    def core_copy(w, g):
        mine = gath[w][g].at[pl.ds(isl * per, per)]
        return pltpu.make_async_remote_copy(
            src_ref=mine, dst_ref=mine,
            send_sem=c_send.at[w, g], recv_sem=c_recv.at[w, g],
            device_id={"island": mate}, device_id_type=MESH)

    def forward_copy(w, g, o):
        came = gath[w][g].at[pl.ds(y_of(n_y - o) * per, per)]
        return pltpu.make_async_remote_copy(
            src_ref=came, dst_ref=came,
            send_sem=f_send.at[w, g, o], recv_sem=f_recv.at[w, g, o],
            device_id={"island": mate}, device_id_type=MESH)

    def forward(w, g):
        for o in range(1, n_y):
            y_copy(w, g, o).wait_recv()
            forward_copy(w, g, o).start()

    def out_copies(w, g):
        first, last, _ = wins[w]
        made = []
        for k, (r0, r1) in enumerate(pieces(first, last, grid, grid)):
            made.append(pltpu.make_async_copy(
                outv.at[pl.ds(g * per, per), pl.ds(r0, r1 - r0)],
                out_hbm.at[pl.ds(g * per, per), pl.ds(r0, r1 - r0)],
                out_sem.at[w, g, k]))
        return made

    def pick(w, g):
        core_copy(w, g).wait_recv()
        for o in range(1, n_y):
            forward_copy(w, g, o).wait_recv()
        first, last, _ = wins[w]
        for i in range(per):
            q = g * per + i
            came = gath[w][g][migr[0, q] * per + i]
            at = 0
            for r0, r1 in pieces(first, last, grid, grid):
                outv[q, r0:r1, :] = came[at:at + r1 - r0]
                at += r1 - r0
        for copy in out_copies(w, g):
            copy.start()

    arrived = 0
    for w, (first, last, need) in enumerate(wins):
        while arrived <= need:
            for o in range(1, n_in):
                part_copy(arrived, o).wait_recv()
            arrived += 1
        ins = pieces(first - HALO, last + HALO, rows, grid)
        tall = last - first + 2 * HALO

        def slot(i, carry, g):
            q = g * per + i
            place = pos[q]
            u = join([recv[r0 // rows][place, r0 % rows:r0 % rows + r1 - r0, :] for r0, r1 in ins])
            u = u + join([up[q, r0:r1, :] for r0, r1 in ins])
            vx = join([vel[0, r0:r1, :] for r0, r1 in ins])
            vy = join([vel[1, r0:r1, :] for r0, r1 in ins])
            for _ in range(STEPS):
                east = pltpu.roll(u, tall - 1, 0)
                west = pltpu.roll(u, 1, 0)
                north = pltpu.roll(u, 127, 1)
                south = pltpu.roll(u, 1, 1)
                slow = advection * u
                flow = (vx + slow) * (east - west) + (vy + slow) * (north - south)
                u = (1.0 - 4.0 * diffusion) * u + diffusion * ((east + west) + (north + south)) - flow
            gath[w][g][isl * per + i] = u[HALO:tall - HALO]
            return carry

        for g in range(GROUPS):
            lax.fori_loop(0, per, functools.partial(slot, g=g), 0)
            for o in range(1, n_y):
                y_copy(w, g, o).start()
            core_copy(w, g).start()
        if w > 0:
            for g in range(GROUPS):
                forward(w - 1, g)
    for g in range(GROUPS):
        forward(n_win - 1, g)
    for w in range(n_win):
        for g in range(GROUPS):
            pick(w, g)

    for o in range(1, n_in):
        req_copy(o).wait_send()
        for c in range(CHUNKS):
            part_copy(c, o).wait_send()
    for w in range(n_win):
        for g in range(GROUPS):
            core_copy(w, g).wait_send()
            for o in range(1, n_y):
                y_copy(w, g, o).wait_send()
                forward_copy(w, g, o).wait_send()
            for copy in out_copies(w, g):
                copy.wait()


def body(particles, velocity_x, velocity_y, copy_lists, migrants, noise):
    n_in = lax.axis_size("inner")
    n_is = lax.axis_size("island")
    n_y = n_is // CORES
    count, grid, _ = particles.shape
    packed = noise.shape[-1] // 128
    rows = grid // CHUNKS
    per = count // GROUPS
    wins = windows_of(grid)
    dma = pltpu.SemaphoreType.DMA
    f32 = jnp.float32
    scratch = [
        pltpu.VMEM((count, grid, grid), f32),
        pltpu.VMEM((count, packed, 128), f32),
        pltpu.VMEM((count, grid, grid), f32),
        pltpu.VMEM((n_in, 1, 128), jnp.int32),
        pltpu.VMEM((n_in - 1, CAP, grid, grid), f32),
        pltpu.VMEM((2, grid, grid), f32),
        pltpu.VMEM((count, grid, grid), f32),
        pltpu.SMEM((count,), jnp.int32),
    ]
    scratch += [pltpu.VMEM((n_in * CAP, rows, grid), f32) for _ in range(CHUNKS)]
    for first, last, _ in wins:
        scratch += [pltpu.VMEM((n_is * per, last - first, grid), f32) for _ in range(GROUPS)]
    scratch += [
        dma((2,)),
        dma((n_in,)), dma((n_in,)),
        dma((CHUNKS, n_in)), dma((CHUNKS, n_in)),
        dma((len(wins), GROUPS, n_y)), dma((len(wins), GROUPS, n_y)),
        dma((len(wins), GROUPS)), dma((len(wins), GROUPS)),
        dma((len(wins), GROUPS, n_y)), dma((len(wins), GROUPS, n_y)),
        dma((len(wins), GROUPS, 2)),
    ]
    smem = pl.BlockSpec(memory_space=pltpu.SMEM)
    vmem = pl.BlockSpec(memory_space=pltpu.VMEM)
    anyw = pl.BlockSpec(memory_space=pl.ANY)
    return pl.pallas_call(
        functools.partial(kernel, n_in, n_is, count, grid),
        out_shape=jax.ShapeDtypeStruct(particles.shape, f32),
        in_specs=[smem, smem, anyw, vmem, vmem, anyw],
        out_specs=anyw,
        scratch_shapes=scratch,
        compiler_params=pltpu.CompilerParams(
            collective_id=0, has_side_effects=True, vmem_limit_bytes=48 * 1024 * 1024),
    )(copy_lists.reshape(1, count), migrants.reshape(1, count), particles,
      velocity_x, velocity_y, noise.reshape(count, packed, 128))


def solution(mesh):
    placed = (
        P(("island", "inner"), None, None),
        P(),
        P(),
        P(None, None, ("island", "inner")),
        P(None, ("island", "inner")),
        P(None, None, ("island", "inner"), None),
    )
    return jax.shard_map(
        body,
        mesh=mesh,
        in_specs=placed,
        out_specs=P(("island", "inner"), None, None),
        check_vma=False,
    )
```

time: 103 us -> 56.6 us (0.55); the launches traced: 102 us -> 56.3 us
  Pallas kernels: 0 us -> 51 us
  waiting for transfers between devices: 41.9 us -> 0 us
  local copies, waits for them, and re-layouts: 23.6 us -> 5.29 us
  between operations: 14.4 us -> 0.02 us
  other arithmetic: 8.73 us -> 0 us
  blocking collectives: 7.86 us -> 0 us
  starting transfers between devices: 5.13 us -> 0 us
    pallas_call x0 -> x1, Pallas kernels: none -> 51 us  [body(): pl.pallas_call(functools.partial(kernel, n_in, n_is, count, grid), out_sh...]
    all_gather x1 -> x0, waiting for transfers between devices: 31.8 us -> none  [body(): lax.all_gather(states, 'island', axis=0, tiled=True)]
    all_to_all x1 -> x0, waiting for transfers between devices: 10.1 us -> none  [copy_direct(): lax.all_to_all(outgoing, 'inner', split_axis=0, concat_axis=0, tiled=True)]
    unnamed x1 -> x0, blocking collectives: 7.86 us -> none
    mul x2 -> x0, local copies, waits for them, and re-layouts: 6.07 us -> none  [body(): states = states + noise_gain * upsample(noise[0, 0])]
    gather x4 -> x0, local copies, waits for them, and re-layouts: 5.59 us -> none  [the longest x1 2.48 us: select_rows(): taken = jnp.take(piece, jnp.clip(wanted, 0, rows - 1), axis=0)]
    sub x8 -> x0, other arithmetic: 5.44 us -> none  [the longest x6 5.43 us: stencil(): return field + diffusion * laplace - advection * transport]
    all_to_all x1 -> x0, starting transfers between devices: 5.13 us -> none  [copy_direct(): lax.all_to_all(outgoing, 'inner', split_axis=0, concat_axis=0, tiled=True)]
  transfers between devices with their start and end apart: 2 -> 0, of which waited for: 2 -> 0; matrix products, arithmetic and copies ran while one was open for 12% -> 0% of each run, Pallas kernels for 0% -> 0%
where the time goes in v1:
time: 56.6 us; the launch traced here: 56.3 us
  Pallas kernels  51 us (90%)
  local copies, waits for them, and re-layouts  5.29 us (9%)
    pallas_call x1, Pallas kernels, body(): pl.pallas_call(functools.partial(kernel, n_in, n_is, count, grid), out_sh...  51 us
    unnamed x13, local copies, waits for them, and re-layouts  5.29 us

profile of v1, /device:TPU:11, one launch (start us, length us, event | category | flops | bytes accessed | tf_op | source)
XLA Modules:
  0.0 56.3 jit_solution(5094252798841114172)
XLA Ops:
  0.0 0.0 copy-start.4
  0.0 0.0 copy-start.5
  0.0 0.7 %copy-done.4 = s32[1,1,12]{2,1,0:T(1,128)S(1)} copy-done((s32[1,1,12]{2,1,0:T(1,128)S(1)}, s32[1,1,12]{2,1,0:T(1,128)}, u32[]{:S(2)}) %copy-start.4) | copy-done | bytes 72
  0.7 0.0 copy-done.5
  0.7 0.0 copy-start
  0.7 1.1 %copy-done = f32[12,128,128]{2,1,0:T(8,128)S(1)} copy-done((f32[12,128,128]{2,1,0:T(8,128)S(1)}, f32[12,128,128]{2,1,0:T(8,128)}, u32[]{:S(2)}) %copy-start) | copy-done | bytes 786456
  1.8 0.0 copy-start.1
  1.8 0.9 %copy-done.1 = f32[1,1,12,4096]{3,1,2,0:T(1,128)S(1)} copy-done((f32[1,1,12,4096]{3,1,2,0:T(1,128)S(1)}, f32[1,1,12,4096]{3,1,2,0:T(1,128)}, u32[]{:S(2)}) %copy-start.1) | copy-done | bytes 196632
  2.7 0.0 copy-start.2
  2.7 0.8 %copy-done.2 = f32[128,128]{1,0:T(8,128)S(1)} copy-done((f32[128,128]{1,0:T(8,128)S(1)}, f32[128,128]{1,0:T(8,128)}, u32[]{:S(2)}) %copy-start.2) | copy-done | bytes 65560
  3.6 0.0 copy-start.3
  3.6 0.8 %copy-done.3 = f32[128,128]{1,0:T(8,128)S(1)} copy-done((f32[128,128]{1,0:T(8,128)S(1)}, f32[128,128]{1,0:T(8,128)}, u32[]{:S(2)}) %copy-start.3) | copy-done | bytes 65560
  4.4 51.0 %shard_map.64 = f32[12,128,128]{2,1,0:T(8,128)S(1)} custom-call(s32[1,12]{1,0:T(1,128)S(1)} %bitcast.3, s32[1,12]{1,0:T(1,128)S(1)} %copy-done.5, f32[12,128,128]{2,1,0:T(8,128)S(1)} %copy-done, f32[128,128]{1,0:T(8,128)S(1)} %copy-done.2, f32[128,128]{1,0:T(8,128)S(1)} %copy-done.3, f32[12,32,128]{2,1,0:T(8,128)S(1)} %bitcast.2), custom_call_target="tpu_custom_call" | custom-call | tf_op jit(solution)/shard_map/pallas_call | solution.py:306
  55.4 0.9 %copy.8 = f32[12,128,128]{2,1,0:T(8,128)} copy(f32[12,128,128]{2,1,0:T(8,128)S(1)} %shard_map.64) | data formatting | bytes 1572864
Async XLA Ops:
  0.0 0.7 %copy-start.4 = (s32[1,1,12]{2,1,0:T(1,128)S(1)}, s32[1,1,12]{2,1,0:T(1,128)}, u32[]{:S(2)}) copy-start(s32[1,1,12]{2,1,0:T(1,128)} %param.9) | copy-start | bytes 148
  0.0 0.7 %copy-start.5 = (s32[1,12]{1,0:T(1,128)S(1)}, s32[1,12]{1,0:T(1,128)}, u32[]{:S(2)}) copy-start(s32[1,12]{1,0:T(1,128)} %refs_1_.1) | copy-start | bytes 148
  0.7 1.1 %copy-start = (f32[12,128,128]{2,1,0:T(8,128)S(1)}, f32[12,128,128]{2,1,0:T(8,128)}, u32[]{:S(2)}) copy-start(f32[12,128,128]{2,1,0:T(8,128)} %refs_2_.1) | copy-start | bytes 2359300
  1.8 0.9 %copy-start.1 = (f32[1,1,12,4096]{3,1,2,0:T(1,128)S(1)}, f32[1,1,12,4096]{3,1,2,0:T(1,128)}, u32[]{:S(2)}) copy-start(f32[1,1,12,4096]{3,1,2,0:T(1,128)} %param.11) | copy-start | bytes 589828
  2.7 0.8 %copy-start.2 = (f32[128,128]{1,0:T(8,128)S(1)}, f32[128,128]{1,0:T(8,128)}, u32[]{:S(2)}) copy-start(f32[128,128]{1,0:T(8,128)} %refs_3_.1) | copy-start | bytes 196612
  3.6 0.8 %copy-start.3 = (f32[128,128]{1,0:T(8,128)S(1)}, f32[128,128]{1,0:T(8,128)}, u32[]{:S(2)}) copy-start(f32[128,128]{1,0:T(8,128)} %refs_4_.1) | copy-start | bytes 196612

commit v2 on v1

--- a/solution.py
+++ b/solution.py
@@ -43,6 +43,16 @@
 
 def join(parts):
     return parts[0] if len(parts) == 1 else jnp.concatenate(parts, axis=0)
+
+
+def step(u, vx, vy):
+    east = pltpu.roll(u, u.shape[0] - 1, 0)
+    west = pltpu.roll(u, 1, 0)
+    north = pltpu.roll(u, u.shape[1] - 1, 1)
+    south = pltpu.roll(u, 1, 1)
+    slow = advection * u
+    flow = (vx + slow) * (east - west) + (vy + slow) * (north - south)
+    return (1.0 - 4.0 * diffusion) * u + diffusion * ((east + west) + (north + south)) - flow
 
 
 def kernel(n_in, n_is, count, grid, *refs):
@@ -81,9 +91,14 @@
     pl.semaphore_signal(barrier, inc=1, device_id={"island": mate}, device_id_type=MESH)
 
     load_part = pltpu.make_async_copy(part_hbm, part, load_sem.at[0])
-    load_nz = pltpu.make_async_copy(noise_hbm, nz, load_sem.at[1])
+    loads = [
+        pltpu.make_async_copy(noise_hbm, nz, load_sem.at[1]),
+        pltpu.make_async_copy(vx_ref, vel.at[0], load_sem.at[2]),
+        pltpu.make_async_copy(vy_ref, vel.at[1], load_sem.at[3]),
+    ]
     load_part.start()
-    load_nz.start()
+    for load in loads:
+        load.start()
 
     lane = lax.broadcasted_iota(jnp.int32, (1, 128), 1)
     ids = [lists[0, q] for q in range(count)]
@@ -142,9 +157,10 @@
         for o in range(1, n_in):
             part_copy(c, o).start()
 
-    vel[0] = advection * vx_ref[...]
-    vel[1] = advection * vy_ref[...]
-    load_nz.wait()
+    for load in loads:
+        load.wait()
+    for k in (0, 1):
+        vel[k] = advection * vel[k]
     from_lane = lax.broadcasted_iota(jnp.int32, (128, 128), 0)
     to_lane = lax.broadcasted_iota(jnp.int32, (128, 128), 1)
     spread = [(from_lane == half * 64 + to_lane // 2).astype(jnp.float32) for half in (0, 1)]
@@ -221,26 +237,19 @@
         ins = pieces(first - HALO, last + HALO, rows, grid)
         tall = last - first + 2 * HALO
 
-        def slot(i, carry, g):
-            q = g * per + i
-            place = pos[q]
-            u = join([recv[r0 // rows][place, r0 % rows:r0 % rows + r1 - r0, :] for r0, r1 in ins])
-            u = u + join([up[q, r0:r1, :] for r0, r1 in ins])
-            vx = join([vel[0, r0:r1, :] for r0, r1 in ins])
-            vy = join([vel[1, r0:r1, :] for r0, r1 in ins])
+        vx = join([vel[0, r0:r1, :] for r0, r1 in ins])
+        vy = join([vel[1, r0:r1, :] for r0, r1 in ins])
+        for g in range(GROUPS):
+            fields = []
+            for i in range(per):
+                q = g * per + i
+                place = pos[q]
+                u = join([recv[r0 // rows][place, r0 % rows:r0 % rows + r1 - r0, :] for r0, r1 in ins])
+                fields.append(u + join([up[q, r0:r1, :] for r0, r1 in ins]))
             for _ in range(STEPS):
-                east = pltpu.roll(u, tall - 1, 0)
-                west = pltpu.roll(u, 1, 0)
-                north = pltpu.roll(u, 127, 1)
-                south = pltpu.roll(u, 1, 1)
-                slow = advection * u
-                flow = (vx + slow) * (east - west) + (vy + slow) * (north - south)
-                u = (1.0 - 4.0 * diffusion) * u + diffusion * ((east + west) + (north + south)) - flow
-            gath[w][g][isl * per + i] = u[HALO:tall - HALO]
-            return carry
-
-        for g in range(GROUPS):
-            lax.fori_loop(0, per, functools.partial(slot, g=g), 0)
+                fields = [step(u, vx, vy) for u in fields]
+            for i, u in enumerate(fields):
+                gath[w][g][isl * per + i] = u[HALO:tall - HALO]
             for o in range(1, n_y):
                 y_copy(w, g, o).start()
             core_copy(w, g).start()
@@ -292,7 +301,7 @@
     for first, last, _ in wins:
         scratch += [pltpu.VMEM((n_is * per, last - first, grid), f32) for _ in range(GROUPS)]
     scratch += [
-        dma((2,)),
+        dma((4,)),
         dma((n_in,)), dma((n_in,)),
         dma((CHUNKS, n_in)), dma((CHUNKS, n_in)),
         dma((len(wins), GROUPS, n_y)), dma((len(wins), GROUPS, n_y)),
@@ -301,12 +310,11 @@
         dma((len(wins), GROUPS, 2)),
     ]
     smem = pl.BlockSpec(memory_space=pltpu.SMEM)
-    vmem = pl.BlockSpec(memory_space=pltpu.VMEM)
-    anyw = pl.BlockSpec(memory_space=pl.ANY)
+    anyw = pl.BlockSpec(memory_space=pltpu.HBM)
     return pl.pallas_call(
         functools.partial(kernel, n_in, n_is, count, grid),
         out_shape=jax.ShapeDtypeStruct(particles.shape, f32),
-        in_specs=[smem, smem, anyw, vmem, vmem, anyw],
+        in_specs=[smem, smem, anyw, anyw, anyw, anyw],
         out_specs=anyw,
         scratch_shapes=scratch,
         compiler_params=pltpu.CompilerParams(

time: 56.6 us -> 52.3 us (0.924)
  Pallas kernels: 51 us -> 46.7 us
    pallas_call x1, Pallas kernels: 51 us -> 46.7 us  [body(): pl.pallas_call(functools.partial(kernel, n_in, n_is, count, grid), out_sh...]
where the time goes in v2:
time: 52.3 us; the launch traced here: 52 us
  Pallas kernels  46.7 us (89%)
  local copies, waits for them, and re-layouts  5.29 us (10%)
    pallas_call x1, Pallas kernels, body(): pl.pallas_call(functools.partial(kernel, n_in, n_is, count, grid), out_sh...  46.7 us
    unnamed x13, local copies, waits for them, and re-layouts  5.29 us

profile of v2, /device:TPU:11, one launch (start us, length us, event | category | flops | bytes accessed | tf_op | source)
XLA Modules:
  0.0 52.0 jit_solution(7393477253194351251)
XLA Ops:
  0.0 0.0 copy-start.4
  0.0 0.0 copy-start.5
  0.0 0.7 %copy-done.4 = s32[1,1,12]{2,1,0:T(1,128)S(1)} copy-done((s32[1,1,12]{2,1,0:T(1,128)S(1)}, s32[1,1,12]{2,1,0:T(1,128)}, u32[]{:S(2)}) %copy-start.4) | copy-done | bytes 72
  0.7 0.0 copy-done.5
  0.7 0.0 copy-start
  0.7 1.1 %copy-done = f32[12,128,128]{2,1,0:T(8,128)S(1)} copy-done((f32[12,128,128]{2,1,0:T(8,128)S(1)}, f32[12,128,128]{2,1,0:T(8,128)}, u32[]{:S(2)}) %copy-start) | copy-done | bytes 786456
  1.8 0.0 copy-start.1
  1.8 0.9 %copy-done.1 = f32[1,1,12,4096]{3,1,2,0:T(1,128)S(1)} copy-done((f32[1,1,12,4096]{3,1,2,0:T(1,128)S(1)}, f32[1,1,12,4096]{3,1,2,0:T(1,128)}, u32[]{:S(2)}) %copy-start.1) | copy-done | bytes 196632
  2.7 0.0 copy-start.2
  2.7 0.8 %copy-done.2 = f32[128,128]{1,0:T(8,128)S(1)} copy-done((f32[128,128]{1,0:T(8,128)S(1)}, f32[128,128]{1,0:T(8,128)}, u32[]{:S(2)}) %copy-start.2) | copy-done | bytes 65560
  3.6 0.0 copy-start.3
  3.6 0.8 %copy-done.3 = f32[128,128]{1,0:T(8,128)S(1)} copy-done((f32[128,128]{1,0:T(8,128)S(1)}, f32[128,128]{1,0:T(8,128)}, u32[]{:S(2)}) %copy-start.3) | copy-done | bytes 65560
  4.4 46.7 %shard_map.64 = f32[12,128,128]{2,1,0:T(8,128)S(1)} custom-call(s32[1,12]{1,0:T(1,128)S(1)} %bitcast.3, s32[1,12]{1,0:T(1,128)S(1)} %copy-done.5, f32[12,128,128]{2,1,0:T(8,128)S(1)} %copy-done, f32[128,128]{1,0:T(8,128)S(1)} %copy-done.2, f32[128,128]{1,0:T(8,128)S(1)} %copy-done.3, f32[12,32,128]{2,1,0:T(8,128)S(1)} %bitcast.2), custom_call_target="tpu_custom_call" | custom-call | tf_op jit(solution)/shard_map/pallas_call | solution.py:314
  51.1 0.9 %copy.8 = f32[12,128,128]{2,1,0:T(8,128)} copy(f32[12,128,128]{2,1,0:T(8,128)S(1)} %shard_map.64) | data formatting | bytes 1572864
Async XLA Ops:
  0.0 0.7 %copy-start.4 = (s32[1,1,12]{2,1,0:T(1,128)S(1)}, s32[1,1,12]{2,1,0:T(1,128)}, u32[]{:S(2)}) copy-start(s32[1,1,12]{2,1,0:T(1,128)} %param.9) | copy-start | bytes 148
  0.0 0.7 %copy-start.5 = (s32[1,12]{1,0:T(1,128)S(1)}, s32[1,12]{1,0:T(1,128)}, u32[]{:S(2)}) copy-start(s32[1,12]{1,0:T(1,128)} %refs_1_.1) | copy-start | bytes 148
  0.7 1.1 %copy-start = (f32[12,128,128]{2,1,0:T(8,128)S(1)}, f32[12,128,128]{2,1,0:T(8,128)}, u32[]{:S(2)}) copy-start(f32[12,128,128]{2,1,0:T(8,128)} %refs_2_.1) | copy-start | bytes 2359300
  1.8 0.9 %copy-start.1 = (f32[1,1,12,4096]{3,1,2,0:T(1,128)S(1)}, f32[1,1,12,4096]{3,1,2,0:T(1,128)}, u32[]{:S(2)}) copy-start(f32[1,1,12,4096]{3,1,2,0:T(1,128)} %param.11) | copy-start | bytes 589828
  2.7 0.8 %copy-start.2 = (f32[128,128]{1,0:T(8,128)S(1)}, f32[128,128]{1,0:T(8,128)}, u32[]{:S(2)}) copy-start(f32[128,128]{1,0:T(8,128)} %refs_3_.1) | copy-start | bytes 196612
  3.6 0.8 %copy-start.3 = (f32[128,128]{1,0:T(8,128)S(1)}, f32[128,128]{1,0:T(8,128)}, u32[]{:S(2)}) copy-start(f32[128,128]{1,0:T(8,128)} %refs_4_.1) | copy-start | bytes 196612

commit v3 on v2

--- a/solution.py
+++ b/solution.py
@@ -318,7 +318,7 @@
         out_specs=anyw,
         scratch_shapes=scratch,
         compiler_params=pltpu.CompilerParams(
-            collective_id=0, has_side_effects=True, vmem_limit_bytes=48 * 1024 * 1024),
+            collective_id=0, has_side_effects=True, vmem_limit_bytes=67043328),
     )(copy_lists.reshape(1, count), migrants.reshape(1, count), particles,
       velocity_x, velocity_y, noise.reshape(count, packed, 128))
 

time: 52.3 us -> 49.5 us (0.946)
  local copies, waits for them, and re-layouts: 5.29 us -> 2.06 us
  Pallas kernels: 46.7 us -> 47.3 us
    unnamed x13 -> x1, local copies, waits for them, and re-layouts: 5.29 us -> 2.06 us
    pallas_call x1, Pallas kernels: 46.7 us -> 47.3 us  [body(): pl.pallas_call(functools.partial(kernel, n_in, n_is, count, grid), out_sh...]
where the time goes in v3:
time: 49.5 us; the launch traced here: 49.4 us
  Pallas kernels  47.3 us (96%)
  local copies, waits for them, and re-layouts  2.06 us (4%)
    pallas_call x1, Pallas kernels, body(): pl.pallas_call(functools.partial(kernel, n_in, n_is, count, grid), out_sh...  47.3 us
    unnamed x1, local copies, waits for them, and re-layouts  2.06 us

profile of v3, /device:TPU:11, one launch (start us, length us, event | category | flops | bytes accessed | tf_op | source)
XLA Modules:
  0.0 49.4 jit_solution(3624856463921533997)
XLA Ops:
  0.0 47.3 %shard_map.64 = f32[12,128,128]{2,1,0:T(8,128)} custom-call(s32[1,12]{1,0:T(1,128)} %bitcast.3, s32[1,12]{1,0:T(1,128)} %refs_1_.1, f32[12,128,128]{2,1,0:T(8,128)} %refs_2_.1, f32[128,128]{1,0:T(8,128)} %refs_3_.1, f32[128,128]{1,0:T(8,128)} %refs_4_.1, f32[12,32,128]{2,1,0:T(8,128)} %bitcast.2), custom_call_target="tpu_custom_call" | custom-call | tf_op jit(solution)/shard_map/pallas_call | solution.py:314
  47.3 2.1 %copy.8 = f32[12,128,128]{2,1,0:T(8,128)} copy(f32[12,128,128]{2,1,0:T(8,128)} %shard_map.64) | data formatting | bytes 1572864

commit v4 on v3

--- a/solution.py
+++ b/solution.py
@@ -256,11 +256,13 @@
         if w > 0:
             for g in range(GROUPS):
                 forward(w - 1, g)
+    for w in range(n_win - 1):
+        for g in range(GROUPS):
+            pick(w, g)
     for g in range(GROUPS):
         forward(n_win - 1, g)
-    for w in range(n_win):
-        for g in range(GROUPS):
-            pick(w, g)
+    for g in range(GROUPS):
+        pick(n_win - 1, g)
 
     for o in range(1, n_in):
         req_copy(o).wait_send()

time: 49.5 us -> 49.5 us (level)
  no operation moved by 1% of the time
where the time goes in v4:
time: 49.5 us; the launch traced here: 49.4 us
  Pallas kernels  47.3 us (96%)
  local copies, waits for them, and re-layouts  2.06 us (4%)
    pallas_call x1, Pallas kernels, body(): pl.pallas_call(functools.partial(kernel, n_in, n_is, count, grid), out_sh...  47.3 us
    unnamed x1, local copies, waits for them, and re-layouts  2.06 us

profile of v4, /device:TPU:11, one launch (start us, length us, event | category | flops | bytes accessed | tf_op | source)
XLA Modules:
  0.0 49.4 jit_solution(6350635033106661470)
XLA Ops:
  0.0 47.3 %shard_map.64 = f32[12,128,128]{2,1,0:T(8,128)} custom-call(s32[1,12]{1,0:T(1,128)} %bitcast.3, s32[1,12]{1,0:T(1,128)} %refs_1_.1, f32[12,128,128]{2,1,0:T(8,128)} %refs_2_.1, f32[128,128]{1,0:T(8,128)} %refs_3_.1, f32[128,128]{1,0:T(8,128)} %refs_4_.1, f32[12,32,128]{2,1,0:T(8,128)} %bitcast.2), custom_call_target="tpu_custom_call" | custom-call | tf_op jit(solution)/shard_map/pallas_call | solution.py:316
  47.3 2.1 %copy.8 = f32[12,128,128]{2,1,0:T(8,128)} copy(f32[12,128,128]{2,1,0:T(8,128)} %shard_map.64) | data formatting | bytes 1572864
